TPU v7x, 256 devices: a whole 4x4x8 slice. The times are simulated.
256 devices in a mesh: ctx: 8 (over z_hi, core), exp: 32 (over x, z_lo, y).
Axes of the slice: x: 4, y: 4, z: 8 (z_hi: 4, z_lo: 2; z = z_hi * 2 + z_lo), core: 2. Of those that a mesh axis runs over, the one named last changes fastest.
Arguments:
- queries: bfloat16 [4096, 4096], P('ctx', 'exp'), may hold values from -8 to 8
- doc_keys: bfloat16 [8192, 4096], P('ctx', 'exp'), may hold values from -8 to 8
- doc_values: bfloat16 [8192, 4096], P('ctx', 'exp'), may hold values from -6 to 6
- residual: bfloat16 [4096, 4096], P(('ctx', 'exp')), may hold values from -3 to 3
- out_weight: bfloat16 [4096, 4096], P('exp'), may hold values from -0.09375 to 0.09375
- norm_gain: float32 [4096], replicated, may hold values from 0.1 to 1.9
- expert_ids: int32 [4096, 1], P(('ctx', 'exp')), may hold values from 0 to 7; in each aligned block of 16 rows (0 to 15, 16 to 31, ...) at most 4 rows name the same one
- gate_up: bfloat16 [32, 4096, 5120], P('exp', None, 'ctx'), may hold values from -0.09375 to 0.09375
- down_weight: bfloat16 [32, 2560, 4096], P('exp', 'ctx'), may hold values from -0.0625 to 0.0625
Outputs:
- attended: bfloat16 [4096, 4096], P(('ctx', 'exp'))
- expert_out: bfloat16 [4096, 4096], P(('ctx', 'exp'))
Inputs may be any that keep to these rules, and one draw needn't show every extreme that they name: `expert_ids`: in each aligned block of 16 tokens, the rows of one device, no expert is named more than 4 times.
All inputs are finite; a program needn't handle non-finite values.
Results may differ from a plain program's by a relative error of at most 0.033.
Values may be sent and summed in bfloat16 or wider, within the bound.
No kernel may reach another device: no remote copies, remote signals or barrier semaphores. Data moves between devices by JAX's collectives and lax.ppermute only.
A program may use at most 128 MiB of HBM per device.

v0:
```python
import jax
import jax.numpy as jnp
from jax import lax
from jax.sharding import PartitionSpec as P

DH = 64
QUARTERS = 4


def score_rows(query_rows, key_rows, head_count):
    query_split = query_rows.reshape(query_rows.shape[0], head_count, -1)
    key_split = key_rows.reshape(key_rows.shape[0], head_count, -1)
    factor = query_split.shape[2] ** (-0.5)
    return (
        jnp.einsum("qhd,khd->qhk", query_split, key_split, preferred_element_type=jnp.float32)
        * factor
    )


def weigh_rows(weights, value_rows, head_count):
    value_split = value_rows.reshape(value_rows.shape[0], head_count, -1)
    return jnp.einsum(
        "qhk,khd->qhd",
        weights.astype(jnp.bfloat16),
        value_split,
        preferred_element_type=jnp.float32,
    )


def on_device(
    queries, doc_keys, doc_values, residual, out_weight, norm_gain, expert_ids, gate_up, down_weight
):
    head_count = queries.shape[1] // DH
    query_count = queries.shape[0]
    row_top = jnp.full((query_count, head_count), -jnp.inf, jnp.float32)
    row_total = jnp.zeros((query_count, head_count), jnp.float32)
    weighted = jnp.zeros((query_count, head_count, DH), jnp.float32)
    scores = score_rows(queries, lax.all_gather(doc_keys, "ctx", axis=0, tiled=True), head_count)
    new_top = jnp.max(scores, axis=2)
    decay_now = jnp.exp(row_top - new_top)
    weights = jnp.exp(scores - new_top[:, :, None])
    row_total = row_total * decay_now + jnp.sum(weights, axis=2)
    weighted = weighted * decay_now[:, :, None] + weigh_rows(
        weights, lax.all_gather(doc_values, "ctx", axis=0, tiled=True), head_count
    )
    row_top, row_total, weighted = (new_top, row_total, weighted)
    context = (
        (weighted / row_total[:, :, None])
        .reshape(query_count, head_count * DH)
        .astype(jnp.bfloat16)
    )
    row_count = residual.shape[0]
    mixed_heads = lax.psum_scatter(
        jnp.dot(context, out_weight, preferred_element_type=jnp.float32).astype(jnp.bfloat16),
        "exp",
        scatter_dimension=0,
        tiled=True,
    ).astype(jnp.float32)
    attended = lax.optimization_barrier(
        (residual.astype(jnp.float32) + mixed_heads).astype(jnp.bfloat16)
    )
    widened = attended.astype(jnp.float32)
    normed = (
        widened * lax.rsqrt(jnp.mean(widened * widened, axis=1, keepdims=True) + 1e-06) * norm_gain
    ).astype(jnp.bfloat16)
    routes = expert_ids[:, 0]
    positions = jnp.arange(row_count, dtype=jnp.int32)
    earlier = (routes[:, None] == routes[None, :]) & (positions[:, None] > positions[None, :])
    slot_rank = jnp.sum(earlier.astype(jnp.int32), axis=1)
    targets = lax.axis_size("exp")
    held_experts = targets // QUARTERS
    capacity = 2 * row_count // held_experts
    target_expert = jnp.arange(targets, dtype=jnp.int32) // QUARTERS
    slot_range = jnp.arange(capacity, dtype=jnp.int32)
    chosen = (routes[None, None, :] == target_expert[:, None, None]) & (
        slot_rank[None, None, :] == slot_range[None, :, None]
    )
    outgoing = jnp.einsum(
        "ekt,td->ekd", chosen.astype(jnp.bfloat16), normed, preferred_element_type=jnp.float32
    ).astype(jnp.bfloat16)
    incoming = lax.all_to_all(outgoing, "exp", split_axis=0, concat_axis=0, tiled=True)
    stacked = incoming.reshape(targets * capacity, incoming.shape[2])
    slice_width = down_weight.shape[1]
    gate_and_up = jnp.dot(
        lax.all_gather(stacked, "ctx", axis=0, tiled=True),
        gate_up[0],
        preferred_element_type=jnp.float32,
    )
    hidden = (jax.nn.silu(gate_and_up[:, :slice_width]) * gate_and_up[:, slice_width:]).astype(
        jnp.bfloat16
    )
    quarter_sums = lax.psum_scatter(
        jnp.dot(hidden, down_weight[0], preferred_element_type=jnp.float32).astype(jnp.bfloat16),
        "ctx",
        scatter_dimension=0,
        tiled=True,
    ).astype(jnp.float32)
    returned = lax.all_to_all(
        quarter_sums.reshape(targets, capacity, -1).astype(jnp.bfloat16),
        "exp",
        split_axis=0,
        concat_axis=0,
        tiled=True,
    ).astype(jnp.float32)
    senders = routes[:, None] * QUARTERS + jnp.arange(QUARTERS, dtype=jnp.int32)[None, :]
    expert_sum = jnp.sum(returned[senders, slot_rank[:, None]], axis=1)
    return (attended, expert_sum.astype(jnp.bfloat16))


def solution(mesh):
    return jax.shard_map(
        on_device,
        mesh=mesh,
        in_specs=(
            P("ctx", "exp"),
            P("ctx", "exp"),
            P("ctx", "exp"),
            P(("ctx", "exp"), None),
            P("exp", None),
            P(),
            P(("ctx", "exp"), None),
            P("exp", None, "ctx"),
            P("exp", "ctx", None),
        ),
        out_specs=(P(("ctx", "exp"), None), P(("ctx", "exp"), None)),
        check_vma=False,
    )
```

profile of v0, /device:TPU:8, one launch (start us, length us, event | category | flops | bytes accessed | tf_op | source)
XLA Modules:
  0.0 540.4 jit_solution(8661302534526715291)
XLA Ops:
  7.2 0.7 all-gather.4.cloned.1.call-update
  8.0 0.7 all-gather.6.cloned.1.call-update
  8.7 1.0 copy.26
  9.7 39.3 %all-gather.4.cloned.1.call-done = bf16[8192,128]{1,0:T(8,128)(2,1)} async-done(((bf16[1024,128]{1,0:T(8,128)(2,1)}), bf16[8192,128]{1,0:T(8,128)(2,1)}) %all-gather.4.cloned.1.call-update) | async-done | bytes 2097168 | tf_op jit(solution)/shard_map/all_gather | solution.py:38
  49.0 4.1 copy.25
  53.1 15.2 %bitcast_reduce_fusion = (f32[512,2]{0,1:T(2,128)S(1)}, f32[2,8192,512]{2,1,0:T(8,128)}) fusion(bf16[8192,2,64]{0,2,1:T(8,128)(2,1)} %bitcast.51, bf16[512,2,64]{0,2,1:T(8,128)(2,1)S(1)} %bitcast.53), kind=kOutput, calls=%fused_computation.2 | convolution fusion | flops 1090518016 | bytes 35786752 | tf_op jit(solution)/shard_map/qhd,khd->qhk/dot_general | solution.py:15
  68.4 15.3 %fusion.1 = f32[512,2]{0,1:T(2,128)S(1)} fusion(f32[2,8192,512]{2,1,0:T(8,128)} %get-tuple-element.5, f32[512,2]{0,1:T(2,128)S(1)} %get-tuple-element.4), kind=kLoop, calls=%fused_computation.4 | loop fusion | flops 25164800 | bytes 33562624 | tf_op jit(solution)/shard_map/reduce_sum | solution.py:42
  83.7 1.8 all-gather.6.cloned.1.call-done
  85.4 4.1 copy.27
  89.6 14.1 %fusion.18 = bf16[512,2,64]{0,2,1:T(8,128)(2,1)S(1)} fusion(bf16[8192,2,64]{0,2,1:T(8,128)(2,1)} %bitcast.50, f32[2,8192,512]{2,1,0:T(8,128)} %get-tuple-element.5, f32[512,2]{0,1:T(2,128)S(1)} %get-tuple-element.4, f32[512,2]{0,1:T(2,128)S(1)} %get-tuple-element.3, f32[512,2]{0,1:T(2,128)S(1)} %get-tuple-element.2), kind=kOutput, calls=%fused_computation.18 | convolution fusion | flops 1099104256 | bytes 35794944 | tf_op jit(solution)/shard_map/qhk,khd->qhd/dot_general | solution.py:22
  103.7 3.2 convolution_convert_fusion.1
  107.0 0.2 convert_reduce_fusion
  107.3 166.1 %reduce-scatter.3.cloned.1.call-done = bf16[16,4096]{1,0:T(8,128)(2,1)} async-done(((bf16[512,4096]{1,0:T(8,128)(2,1)}), bf16[16,4096]{1,0:T(8,128)(2,1)}) %reduce-scatter.3.cloned.1.call-update) | async-done | bytes 131088 | tf_op jit(solution)/shard_map/reduce_scatter | solution.py:53
  273.4 0.9 add_convert_fusion
  274.3 0.1 fusion.23
  274.5 0.6 convolution_convert_fusion.2
  275.0 0.8 copy.29
  275.9 21.7 %all_to_all.10 = bf16[32,4,4096]{2,1,0:T(4,128)(2,1)} all-to-all(bf16[32,4,4096]{2,1,0:T(4,128)(2,1)S(1)} %copy.29), channel_id=1, replica_groups=mesh['ctx'=8,'exp'=32] {'exp'}, dimensions={0} | all-to-all | bytes 2097152 | tf_op jit(solution)/shard_map/all_to_all | solution.py:81
  297.6 2.2 reshape.167
  299.8 0.2 reduce-scatter.5.cloned.1.call-start
  300.0 80.6 %all-gather.8.cloned.1.call-done = bf16[1024,4096]{1,0:T(8,128)(2,1)} async-done(((bf16[128,4096]{1,0:T(8,128)(2,1)}), bf16[1024,4096]{1,0:T(8,128)(2,1)}) %all-gather.8.cloned.1.call-update) | async-done | bytes 8388624 | tf_op jit(solution)/shard_map/all_gather | solution.py:85
  380.6 9.6 %fusion.5 = f32[1024,640]{0,1:T(8,128)S(1)} fusion(bf16[1024,4096]{1,0:T(8,128)(2,1)} %all-gather.8.cloned.1.call-done, bf16[1,4096,640]{2,1,0:T(8,128)(2,1)} %param.16), kind=kOutput, calls=%fused_computation.9 | convolution fusion | flops 5368709120 | bytes 16252928 | tf_op jit(solution)/shard_map/dot_general | solution.py:84
  390.3 7.0 %convolution_convert_fusion = bf16[1024,4096]{1,0:T(8,128)(2,1)} fusion(bf16[1,320,4096]{2,1,0:T(8,128)(2,1)S(1)} %copy-done, f32[1024,640]{0,1:T(8,128)S(1)} %fusion.5), kind=kOutput, calls=%fused_computation.7 | convolution fusion | flops 2690514944 | bytes 13631488 | tf_op jit(solution)/shard_map/dot_general | solution.py:93
  397.3 100.7 %reduce-scatter.5.cloned.1.call-done = bf16[128,4096]{1,0:T(8,128)(2,1)} async-done(((bf16[1024,4096]{1,0:T(8,128)(2,1)}), bf16[128,4096]{1,0:T(8,128)(2,1)}) %reduce-scatter.5.cloned.1.call-update) | async-done | bytes 1048592 | tf_op jit(solution)/shard_map/reduce_scatter | solution.py:92
  497.9 2.2 convert_element_type.64
  500.1 9.8 %all-to-all-start.1 = ((bf16[32,4,4096]{2,1,0:T(4,128)(2,1)}), bf16[32,4,4096]{2,1,0:T(4,128)(2,1)}, u32[]{:S(2)}, u32[]{:S(2)}) async-start(bf16[32,4,4096]{2,1,0:T(4,128)(2,1)} %convert_element_type.64), calls=%async_computation.3 | async-start | bytes 2097152 | tf_op jit(solution)/shard_map/all_to_all | solution.py:98
  510.0 0.1 reshape.168
  510.1 12.5 %all-to-all-done.1 = bf16[32,4,4096]{2,1,0:T(4,128)(2,1)} async-done(((bf16[32,4,4096]{2,1,0:T(4,128)(2,1)}), bf16[32,4,4096]{2,1,0:T(4,128)(2,1)}, u32[]{:S(2)}, u32[]{:S(2)}) %all-to-all-start.1) | async-done | bytes 1048608 | tf_op jit(solution)/shard_map/all_to_all | solution.py:98
  522.6 2.8 convert_element_type.65
  525.4 3.4 gather_fusion
  528.9 2.5 reshape.171
  531.4 2.5 reduce_sum.39
  (27 shorter events, 0.4 us)
Async XLA Ops:
  7.2 383.1 %copy-start = (bf16[1,320,4096]{2,1,0:T(8,128)(2,1)S(1)}, bf16[1,320,4096]{2,1,0:T(8,128)(2,1)}, u32[]{:S(2)}) copy-start(bf16[1,320,4096]{2,1,0:T(8,128)(2,1)} %param.17) | copy-start | bytes 7864324
  7.2 41.8 %all-gather.4.cloned.1.call-start = ((), (), s32[]{:S(2)}) async-start(), calls=%async_computation.4 | async-start | bytes 2359296 | tf_op jit(solution)/shard_map/all_gather | solution.py:38
  7.9 77.5 %all-gather.6.cloned.1.call-start = ((), (), s32[]{:S(2)}) async-start(), calls=%async_computation.5 | async-start | bytes 2359296 | tf_op jit(solution)/shard_map/all_gather | solution.py:44
  8.7 264.7 %reduce-scatter.3.cloned.1.call-start = ((), (), s32[]{:S(2)}) async-start(), calls=%async_computation.6 | async-start | bytes 4325376 | tf_op jit(solution)/shard_map/reduce_scatter | solution.py:53
  89.6 14.1 %copy-start.2 = (bf16[128,4096]{1,0:T(8,128)(2,1)S(1)}, bf16[128,4096]{1,0:T(8,128)(2,1)}, u32[]{:S(2)}) copy-start(bf16[128,4096]{1,0:T(8,128)(2,1)} %param.13) | copy-start | bytes 3145732
  103.7 3.3 copy-start.5
  103.7 169.7 %copy-start.3 = (bf16[16,4096]{1,0:T(8,128)(2,1)S(1)}, bf16[16,4096]{1,0:T(8,128)(2,1)}, u32[]{:S(2)}) copy-start(bf16[16,4096]{1,0:T(8,128)(2,1)} %param.12) | copy-start | bytes 393220
  106.9 167.6 %copy-start.4 = (f32[4096]{0:T(1024)S(1)}, f32[4096]{0:T(1024)}, u32[]{:S(2)}) copy-start(f32[4096]{0:T(1024)} %param.14) | copy-start | bytes 49156
  106.9 273.7 %all-gather.8.cloned.1.call-start = ((), (), s32[]{:S(2)}) async-start(), calls=%async_computation.7 | async-start | bytes 9437184 | tf_op jit(solution)/shard_map/all_gather | solution.py:85
  274.3 25.5 %copy-start.1 = (bf16[16,4096]{1,0:T(8,128)(2,1)}, bf16[16,4096]{1,0:T(8,128)(2,1)S(1)}, u32[]{:S(2)}) copy-start(bf16[16,4096]{1,0:T(8,128)(2,1)S(1)} %add_convert_fusion) | copy-start | bytes 393220
  299.8 198.1 %reduce-scatter.5.cloned.1.call-start = ((), (), s32[]{:S(2)}) async-start(), calls=%async_computation.8 | async-start | bytes 9437184 | tf_op jit(solution)/shard_map/reduce_scatter | solution.py:92
  500.1 22.5 %all-to-all-start.1 = ((bf16[32,4,4096]{2,1,0:T(4,128)(2,1)}), bf16[32,4,4096]{2,1,0:T(4,128)(2,1)}, u32[]{:S(2)}, u32[]{:S(2)}) async-start(bf16[32,4,4096]{2,1,0:T(4,128)(2,1)} %convert_element_type.64), calls=%async_computation.3 | async-start | bytes 2097152 | tf_op jit(solution)/shard_map/all_to_all | solution.py:98
Sparse Core Ops, SparseCore 0:
  9.8 39.0 all-gather.3
  50.8 34.5 all-gather.5
  107.1 166.2 reduce-scatter.2
  299.9 80.6 all-gather.7
  397.4 100.4 reduce-scatter.4
where the time goes:
time: 541 us; the launch traced here: 540 us
  waiting for transfers between devices  402 us (74%)
  matrix products  49.7 us (9%)
  other arithmetic  22.1 us (4%)
  blocking collectives  21.7 us (4%)
  local copies, waits for them, and re-layouts  20.6 us (4%)
  between operations  13.9 us (3%)
  starting transfers between devices  10.1 us (2%)
    reduce_scatter x1, waiting for transfers between devices, on_device(): lax.psum_scatter(jnp.dot(context, out_weight, preferred_element_type=jnp....  166 us
    reduce_scatter x1, waiting for transfers between devices, on_device(): lax.psum_scatter(jnp.dot(hidden, down_weight[0], preferred_element_type=j...  101 us
    all_gather x1, waiting for transfers between devices, on_device(): lax.all_gather(stacked, 'ctx', axis=0, tiled=True)  80.6 us
    all_gather x1, waiting for transfers between devices, on_device(): lax.all_gather(doc_keys, 'ctx', axis=0, tiled=True)  39.3 us
    all_to_all x1, blocking collectives, on_device(): lax.all_to_all(outgoing, 'exp', split_axis=0, concat_axis=0, tiled=True)  21.7 us
    reduce_sum x1, other arithmetic, on_device(): row_total = row_total * decay_now + jnp.sum(weights, axis=2)  15.3 us
    dot_general x1, matrix products, score_rows(): jnp.einsum('qhd,khd->qhk', query_split, key_split, preferred_element_type...  15.2 us
    dot_general x1, matrix products, weigh_rows(): jnp.einsum('qhk,khd->qhd', weights.astype(jnp.bfloat16), value_split, pre...  14.1 us
  transfers between devices with their start and end apart: 6, of which 6 were waited for; matrix products, arithmetic and copies ran while one was open for 7% of the time, Pallas kernels for 0%

commit v1 on v0

--- a/solution.py
+++ b/solution.py
@@ -82,7 +82,9 @@
     stacked = incoming.reshape(targets * capacity, incoming.shape[2])
     slice_width = down_weight.shape[1]
     gate_and_up = jnp.dot(
-        lax.all_gather(stacked, "ctx", axis=0, tiled=True),
+        jnp.concatenate(
+            lax.all_to_all(jnp.stack([stacked] * lax.axis_size("ctx")), "ctx", 0, 0), axis=0
+        ),
         gate_up[0],
         preferred_element_type=jnp.float32,
     )

time: 541 us -> 645 us (1.19)
  blocking collectives: 21.7 us -> 213 us
  waiting for transfers between devices: 402 us -> 314 us
    all_to_all x0 -> x1, blocking collectives: none -> 192 us  [on_device(): lax.all_to_all(jnp.stack([stacked] * lax.axis_size('ctx')), 'ctx', 0, 0)]
    all_gather x1 -> x0, waiting for transfers between devices: 80.6 us -> none  [on_device(): lax.all_gather(stacked, 'ctx', axis=0, tiled=True)]
    reduce_scatter x1, waiting for transfers between devices: 101 us -> 92.1 us  [on_device(): lax.psum_scatter(jnp.dot(hidden, down_weight[0], preferred_element_type=j...]
  transfers between devices with their start and end apart: 6 -> 5, of which waited for: 6 -> 5; matrix products, arithmetic and copies ran while one was open for 7% -> 6% of each run, Pallas kernels for 0% -> 0%
where the time goes in v1:
time: 645 us; the launch traced here: 644 us
  waiting for transfers between devices  314 us (49%)
  blocking collectives  213 us (33%)
  matrix products  48.3 us (7%)
  local copies, waits for them, and re-layouts  23.3 us (4%)
  other arithmetic  22.1 us (3%)
  between operations  13.9 us (2%)
  starting transfers between devices  9.68 us (2%)
    all_to_all x1, blocking collectives, on_device(): lax.all_to_all(jnp.stack([stacked] * lax.axis_size('ctx')), 'ctx', 0, 0)  192 us
    reduce_scatter x1, waiting for transfers between devices, on_device(): lax.psum_scatter(jnp.dot(context, out_weight, preferred_element_type=jnp....  167 us
    reduce_scatter x1, waiting for transfers between devices, on_device(): lax.psum_scatter(jnp.dot(hidden, down_weight[0], preferred_element_type=j...  92.1 us
    all_gather x1, waiting for transfers between devices, on_device(): lax.all_gather(doc_keys, 'ctx', axis=0, tiled=True)  39.3 us
    all_to_all x1, blocking collectives, on_device(): lax.all_to_all(outgoing, 'exp', split_axis=0, concat_axis=0, tiled=True)  21.1 us
    reduce_sum x1, other arithmetic, on_device(): row_total = row_total * decay_now + jnp.sum(weights, axis=2)  15.3 us
    dot_general x1, matrix products, score_rows(): jnp.einsum('qhd,khd->qhk', query_split, key_split, preferred_element_type...  15.2 us
    dot_general x1, matrix products, weigh_rows(): jnp.einsum('qhk,khd->qhd', weights.astype(jnp.bfloat16), value_split, pre...  14.1 us
  transfers between devices with their start and end apart: 5, of which 5 were waited for; matrix products, arithmetic and copies ran while one was open for 6% of the time, Pallas kernels for 0%

profile of v1, /device:TPU:8, one launch (start us, length us, event | category | flops | bytes accessed | tf_op | source)
XLA Modules:
  0.0 644.0 jit_solution(14036507229472581113)
XLA Ops:
  7.2 0.7 all-gather.3.cloned.1.call-update
  8.0 0.7 all-gather.5.cloned.1.call-update
  8.7 1.0 copy.26
  9.7 39.3 %all-gather.3.cloned.1.call-done = bf16[8192,128]{1,0:T(8,128)(2,1)} async-done(((bf16[1024,128]{1,0:T(8,128)(2,1)}), bf16[8192,128]{1,0:T(8,128)(2,1)}) %all-gather.3.cloned.1.call-update) | async-done | bytes 2097168 | tf_op jit(solution)/shard_map/all_gather | solution.py:38
  49.0 4.1 copy.25
  53.1 15.2 %bitcast_reduce_fusion = (f32[512,2]{0,1:T(2,128)S(1)}, f32[2,8192,512]{2,1,0:T(8,128)}) fusion(bf16[8192,2,64]{0,2,1:T(8,128)(2,1)} %bitcast.52, bf16[512,2,64]{0,2,1:T(8,128)(2,1)S(1)} %bitcast.55), kind=kOutput, calls=%fused_computation.2 | convolution fusion | flops 1090518016 | bytes 35786752 | tf_op jit(solution)/shard_map/qhd,khd->qhk/dot_general | solution.py:15
  68.3 15.3 %fusion.1 = f32[512,2]{0,1:T(2,128)S(1)} fusion(f32[2,8192,512]{2,1,0:T(8,128)} %get-tuple-element.5, f32[512,2]{0,1:T(2,128)S(1)} %get-tuple-element.4), kind=kLoop, calls=%fused_computation.4 | loop fusion | flops 25164800 | bytes 33562624 | tf_op jit(solution)/shard_map/reduce_sum | solution.py:42
  83.6 1.8 all-gather.5.cloned.1.call-done
  85.4 4.1 copy.27
  89.5 14.1 %fusion.18 = bf16[512,2,64]{0,2,1:T(8,128)(2,1)S(1)} fusion(bf16[8192,2,64]{0,2,1:T(8,128)(2,1)} %bitcast.51, f32[2,8192,512]{2,1,0:T(8,128)} %get-tuple-element.5, f32[512,2]{0,1:T(2,128)S(1)} %get-tuple-element.4, f32[512,2]{0,1:T(2,128)S(1)} %get-tuple-element.3, f32[512,2]{0,1:T(2,128)S(1)} %get-tuple-element.2), kind=kOutput, calls=%fused_computation.18 | convolution fusion | flops 1099104256 | bytes 35794944 | tf_op jit(solution)/shard_map/qhk,khd->qhd/dot_general | solution.py:22
  103.7 3.2 convolution_convert_fusion.1
  107.0 0.2 convert_reduce_fusion
  107.2 166.6 %reduce-scatter.3.cloned.1.call-done = bf16[16,4096]{1,0:T(8,128)(2,1)} async-done(((bf16[512,4096]{1,0:T(8,128)(2,1)}), bf16[16,4096]{1,0:T(8,128)(2,1)}) %reduce-scatter.3.cloned.1.call-update) | async-done | bytes 131088 | tf_op jit(solution)/shard_map/reduce_scatter | solution.py:53
  273.8 0.9 add_convert_fusion
  274.8 0.1 fusion.23
  274.9 0.5 copy-done.1
  275.4 0.5 convolution_convert_fusion.2
  276.0 0.8 copy.29
  276.8 21.1 %all_to_all.15 = bf16[32,4,4096]{2,1,0:T(4,128)(2,1)} all-to-all(bf16[32,4,4096]{2,1,0:T(4,128)(2,1)S(1)} %copy.29), channel_id=1, replica_groups=mesh['ctx'=8,'exp'=32] {'exp'}, dimensions={0} | all-to-all | bytes 2097152 | tf_op jit(solution)/shard_map/all_to_all | solution.py:81
  297.9 2.2 stack_reshape.2
  300.1 2.3 stack.3
  302.3 191.9 %all_to_all.16 = bf16[8,128,4096]{2,1,0:T(8,128)(2,1)S(1)} all-to-all(bf16[8,128,4096]{2,1,0:T(8,128)(2,1)S(1)} %stack.3), channel_id=1, replica_groups=mesh['ctx'=8,'exp'=32] {'ctx'}, dimensions={0} | all-to-all | bytes 16777216 | tf_op jit(solution)/shard_map/all_to_all | solution.py:86
  494.3 8.4 %fusion.5 = f32[1024,640]{0,1:T(8,128)S(1)} fusion(bf16[1024,4096]{1,0:T(8,128)(2,1)S(1)} %bitcast.53, bf16[1,4096,640]{2,1,0:T(8,128)(2,1)} %param.16), kind=kOutput, calls=%fused_computation.9 | convolution fusion | flops 5368709120 | bytes 16252928 | tf_op jit(solution)/shard_map/dot_general | solution.py:84
  502.6 6.9 %convolution_convert_fusion = bf16[1024,4096]{1,0:T(8,128)(2,1)} fusion(bf16[1,320,4096]{2,1,0:T(8,128)(2,1)S(1)} %copy-done, f32[1024,640]{0,1:T(8,128)S(1)} %fusion.5), kind=kOutput, calls=%fused_computation.7 | convolution fusion | flops 2690514944 | bytes 13631488 | tf_op jit(solution)/shard_map/dot_general | solution.py:95
  509.6 92.1 %reduce-scatter.5.cloned.1.call-done = bf16[128,4096]{1,0:T(8,128)(2,1)} async-done(((bf16[1024,4096]{1,0:T(8,128)(2,1)}), bf16[128,4096]{1,0:T(8,128)(2,1)}) %reduce-scatter.5.cloned.1.call-update) | async-done | bytes 1048592 | tf_op jit(solution)/shard_map/reduce_scatter | solution.py:94
  601.6 2.2 convert_element_type.64
  603.9 9.5 %all-to-all-start.2 = ((bf16[32,4,4096]{2,1,0:T(4,128)(2,1)}), bf16[32,4,4096]{2,1,0:T(4,128)(2,1)}, u32[]{:S(2)}, u32[]{:S(2)}) async-start(bf16[32,4,4096]{2,1,0:T(4,128)(2,1)} %convert_element_type.64), calls=%async_computation.4 | async-start | bytes 2097152 | tf_op jit(solution)/shard_map/all_to_all | solution.py:100
  613.6 12.6 %all-to-all-done.2 = bf16[32,4,4096]{2,1,0:T(4,128)(2,1)} async-done(((bf16[32,4,4096]{2,1,0:T(4,128)(2,1)}), bf16[32,4,4096]{2,1,0:T(4,128)(2,1)}, u32[]{:S(2)}, u32[]{:S(2)}) %all-to-all-start.2) | async-done | bytes 1048608 | tf_op jit(solution)/shard_map/all_to_all | solution.py:100
  626.2 2.8 convert_element_type.65
  629.0 3.4 gather_fusion
  632.4 2.5 reshape.173
  634.9 2.5 reduce_sum.39
  (26 shorter events, 0.5 us)
Async XLA Ops:
  7.2 495.5 %copy-start = (bf16[1,320,4096]{2,1,0:T(8,128)(2,1)S(1)}, bf16[1,320,4096]{2,1,0:T(8,128)(2,1)}, u32[]{:S(2)}) copy-start(bf16[1,320,4096]{2,1,0:T(8,128)(2,1)} %param.17) | copy-start | bytes 7864324
  7.2 41.8 %all-gather.3.cloned.1.call-start = ((), (), s32[]{:S(2)}) async-start(), calls=%async_computation.5 | async-start | bytes 2359296 | tf_op jit(solution)/shard_map/all_gather | solution.py:38
  7.9 77.5 %all-gather.5.cloned.1.call-start = ((), (), s32[]{:S(2)}) async-start(), calls=%async_computation.6 | async-start | bytes 2359296 | tf_op jit(solution)/shard_map/all_gather | solution.py:44
  8.7 265.1 %reduce-scatter.3.cloned.1.call-start = ((), (), s32[]{:S(2)}) async-start(), calls=%async_computation.7 | async-start | bytes 4325376 | tf_op jit(solution)/shard_map/reduce_scatter | solution.py:53
  89.5 14.1 %copy-start.2 = (bf16[128,4096]{1,0:T(8,128)(2,1)S(1)}, bf16[128,4096]{1,0:T(8,128)(2,1)}, u32[]{:S(2)}) copy-start(bf16[128,4096]{1,0:T(8,128)(2,1)} %param.13) | copy-start | bytes 3145732
  103.6 3.3 copy-start.5
  103.6 170.2 %copy-start.3 = (bf16[16,4096]{1,0:T(8,128)(2,1)S(1)}, bf16[16,4096]{1,0:T(8,128)(2,1)}, u32[]{:S(2)}) copy-start(bf16[16,4096]{1,0:T(8,128)(2,1)} %param.12) | copy-start | bytes 393220
  103.7 171.7 %copy-start.4 = (f32[4096]{0:T(1024)S(1)}, f32[4096]{0:T(1024)}, u32[]{:S(2)}) copy-start(f32[4096]{0:T(1024)} %param.14) | copy-start | bytes 49156
  106.9 494.7 %reduce-scatter.5.cloned.1.call-start = ((), (), s32[]{:S(2)}) async-start(), calls=%async_computation.8 | async-start | bytes 9437184 | tf_op jit(solution)/shard_map/reduce_scatter | solution.py:94
  274.7 0.7 copy-start.1
  603.9 22.3 %all-to-all-start.2 = ((bf16[32,4,4096]{2,1,0:T(4,128)(2,1)}), bf16[32,4,4096]{2,1,0:T(4,128)(2,1)}, u32[]{:S(2)}, u32[]{:S(2)}) async-start(bf16[32,4,4096]{2,1,0:T(4,128)(2,1)} %convert_element_type.64), calls=%async_computation.4 | async-start | bytes 2097152 | tf_op jit(solution)/shard_map/all_to_all | solution.py:100
Sparse Core Ops, SparseCore 0:
  9.8 39.0 all-gather.2
  50.8 34.5 all-gather.4
  107.0 166.7 reduce-scatter.2
  509.7 91.9 reduce-scatter.4
